TPU v7x, 32 devices: a whole 2x2x4 slice. The times are simulated.
32 devices in a mesh: dp: 8 (over y, x, core), mp: 4 (over z).
Axes of the slice: x: 2, y: 2, z: 4, core: 2. Of those that a mesh axis runs over, the one named last changes fastest.
Arguments:
- tokens: bfloat16 [2, 8704, 1024], P(None, ('dp', 'mp')), may hold values from -6 to 6
- seg_ids: int32 [2, 8704], P(None, 'dp'), may hold values from 0 to 1, as said below
- qkv_weight: bfloat16 [3, 1024, 1024], P(None, 'dp', 'mp'), may hold values from -0.25 to 0.25
- qv_bias: bfloat16 [2, 1024], P(None, ('mp', 'dp')), may hold values from -2 to 2
- out_weight: bfloat16 [1024, 1024], P(('mp', 'dp')), may hold values from -0.1875 to 0.1875
- up_weight: bfloat16 [1024, 4096], P('dp', 'mp'), may hold values from -0.1875 to 0.1875
- up_bias: bfloat16 [4096], P(('mp', 'dp')), may hold values from -3 to 3
- down_weight: bfloat16 [4096, 1024], P(('mp', 'dp')), may hold values from -0.09375 to 0.09375
- norm_gain: bfloat16 [4, 1024], P(None, 'dp'), may hold values from 0.099609375 to 1.8984375
- norm_bias: bfloat16 [4, 1024], P(None, 'dp'), may hold values from -2 to 2
- branch_bias: bfloat16 [2, 1024], P(None, 'dp'), may hold values from -3 to 3
- out_grad: bfloat16 [2, 8704, 1024], P(None, ('dp', 'mp')), may hold values from -6 to 6
Outputs:
- layer_out: bfloat16 [2, 8704, 1024], P(None, ('dp', 'mp'))
- input_grad: float32 [2, 8704, 1024], P(None, ('dp', 'mp'))
- qkv_grad: float32 [3, 1024, 1024], P(None, 'dp', 'mp')
- qv_bias_grad: float32 [2, 1024], P(None, ('mp', 'dp'))
- out_weight_grad: float32 [1024, 1024], P(('mp', 'dp'))
- up_weight_grad: float32 [1024, 4096], P('dp', 'mp')
- up_bias_grad: float32 [4096], P(('mp', 'dp'))
- down_weight_grad: float32 [4096, 1024], P(('mp', 'dp'))
- norm_gain_grad: float32 [4, 1024], P(None, 'dp')
- norm_bias_grad: float32 [4, 1024], P(None, 'dp')
- branch_bias_grad: float32 [2, 1024], P(None, 'dp')
Inputs may be any that keep to these rules, and one draw needn't show every extreme that they name: `seg_ids`: each packed row of 1088 tokens holds 1 items numbered 0 upward in order, each of 1024 image codes plus 5 to 64 caption tokens; the rest of the row is padding numbered 1.
All inputs are finite; a program needn't handle non-finite values.
Results may differ from a plain program's by a relative error of at most 0.019.
Values may be sent and summed in bfloat16 or wider, within the bound.
A program may use at most 192 MiB of HBM per device.

v0:
```python
import math
import jax
import jax.numpy as jnp
from jax import lax
from jax.sharding import PartitionSpec as P

HEAD_DIM = 64
ALPHA = 32.0
EPS = 1e-05


def normalize(value, gain, shift):
    mean = jnp.mean(value, axis=-1, keepdims=True)
    centred = value - mean
    variance = jnp.mean(centred * centred, axis=-1, keepdims=True)
    return centred * lax.rsqrt(variance + EPS) * gain + shift


def normalize_back(value, gain, grad):
    mean = jnp.mean(value, axis=-1, keepdims=True)
    centred = value - mean
    variance = jnp.mean(centred * centred, axis=-1, keepdims=True)
    inverse = lax.rsqrt(variance + EPS)
    unit = centred * inverse
    scaled = grad * gain
    grad_in = inverse * (
        scaled
        - jnp.mean(scaled, axis=-1, keepdims=True)
        - unit * jnp.mean(scaled * unit, axis=-1, keepdims=True)
    )
    return (grad_in, jnp.sum(grad * unit, axis=0), jnp.sum(grad, axis=0))


def gelu_exact(value):
    return jax.nn.gelu(value, approximate=False)


def block_mask(seg_row, start, block):
    query_pos = start + jnp.arange(block, dtype=jnp.int32)
    key_pos = jnp.arange(seg_row.shape[0], dtype=jnp.int32)
    seg_block = seg_row[start : start + block]
    return (seg_block[:, None] == seg_row[None, :]) & (key_pos[None, :] <= query_pos[:, None])


def attend_forward(queries, keys, values, seg_row):
    length = queries.shape[0]
    block = length // 4
    results = []
    sums = []
    for part_index in range(4):
        start = part_index * block
        q_block = queries[start : start + block]
        allowed = block_mask(seg_row, start, block)[None]
        scores = jnp.einsum("qhd,khd->hqk", q_block, keys, preferred_element_type=jnp.float32)
        masked = jnp.where(allowed, scores, -1e30)
        top = jnp.max(masked, axis=-1, keepdims=True)
        expo = jnp.exp(ALPHA * (masked - top))
        total = jnp.sum(expo, axis=-1, keepdims=True)
        probs = (expo / total).astype(jnp.bfloat16)
        results.append(
            jnp.einsum("hqk,khd->qhd", probs, values, preferred_element_type=jnp.float32)
        )
        sums.append(ALPHA * top + jnp.log(total))
    return (jnp.concatenate(results, axis=0), jnp.concatenate(sums, axis=1))


def attend_backward(queries, keys, values, seg_row, log_sums, grad_out):
    length = queries.shape[0]
    block = length // 4
    grad_queries = []
    grad_keys = jnp.zeros(keys.shape, jnp.float32)
    grad_values = jnp.zeros(values.shape, jnp.float32)
    for part_index in range(4):
        start = part_index * block
        q_block = queries[start : start + block]
        g_block = grad_out[start : start + block]
        allowed = block_mask(seg_row, start, block)[None]
        scores = jnp.einsum("qhd,khd->hqk", q_block, keys, preferred_element_type=jnp.float32)
        masked = jnp.where(allowed, scores, -1e30)
        probs_full = jnp.exp(ALPHA * masked - log_sums[:, start : start + block])
        probs = probs_full.astype(jnp.bfloat16)
        grad_probs = jnp.einsum("qhd,khd->hqk", g_block, values, preferred_element_type=jnp.float32)
        delta = jnp.sum(probs_full * grad_probs, axis=-1, keepdims=True)
        grad_scores = (ALPHA * probs_full * (grad_probs - delta)).astype(jnp.bfloat16)
        grad_queries.append(
            jnp.einsum("hqk,khd->qhd", grad_scores, keys, preferred_element_type=jnp.float32)
        )
        grad_keys = grad_keys + jnp.einsum(
            "hqk,qhd->khd", grad_scores, q_block, preferred_element_type=jnp.float32
        )
        grad_values = grad_values + jnp.einsum(
            "hqk,qhd->khd", probs, g_block, preferred_element_type=jnp.float32
        )
    return (jnp.concatenate(grad_queries, axis=0), grad_keys, grad_values)


def on_device(
    tokens,
    seg_ids,
    qkv_weight,
    qv_bias,
    out_weight,
    up_weight,
    up_bias,
    down_weight,
    norm_gain,
    norm_bias,
    branch_bias,
    out_grad,
):

    def fetch():
        return (
            lax.all_gather(qkv_weight, "dp", axis=1, tiled=True),
            lax.all_gather(qv_bias, "dp", axis=1, tiled=True),
            lax.all_gather(out_weight, "dp", axis=0, tiled=True),
            lax.all_gather(up_weight, "dp", axis=0, tiled=True),
            lax.all_gather(up_bias, "dp", axis=0, tiled=True),
            lax.all_gather(down_weight, "dp", axis=0, tiled=True),
            lax.all_gather(norm_gain, "dp", axis=1, tiled=True),
            lax.all_gather(norm_bias, "dp", axis=1, tiled=True),
            lax.all_gather(branch_bias, "dp", axis=1, tiled=True),
        )

    scale = 1.0 / (ALPHA * math.sqrt(HEAD_DIM))
    batches = tokens.shape[0]
    length = seg_ids.shape[1]
    share = length // lax.axis_size("mp")
    saved = []
    outputs = []
    for step in range(batches):
        weights = fetch()
        qkv, qv_b, w_out, w_up, b_up, w_down, gains, shifts, branch_b = weights
        gains = gains.astype(jnp.float32)
        shifts = shifts.astype(jnp.float32)
        branch_b = branch_b.astype(jnp.float32)
        qv_b = qv_b.astype(jnp.float32)
        x_rows = tokens[step].astype(jnp.float32)
        seg_row = seg_ids[step]
        normed = normalize(x_rows, gains[0], shifts[0]).astype(jnp.bfloat16)
        hidden_in = lax.all_gather(normed, "mp", axis=0, tiled=True)
        queries = (
            (jnp.dot(hidden_in, qkv[0], preferred_element_type=jnp.float32) + qv_b[0]) * scale
        ).astype(jnp.bfloat16)
        keys = jnp.dot(hidden_in, qkv[1], preferred_element_type=jnp.float32).astype(jnp.bfloat16)
        values = (jnp.dot(hidden_in, qkv[2], preferred_element_type=jnp.float32) + qv_b[1]).astype(
            jnp.bfloat16
        )
        heads = queries.shape[1] // HEAD_DIM
        q_heads = queries.reshape(length, heads, HEAD_DIM)
        k_heads = keys.reshape(length, heads, HEAD_DIM)
        v_heads = values.reshape(length, heads, HEAD_DIM)
        attended, log_sums = attend_forward(q_heads, k_heads, v_heads, seg_row)
        mixed = attended.reshape(length, heads * HEAD_DIM).astype(jnp.bfloat16)

        def out_term(start, count, mixed=mixed, w_out=w_out):
            return jnp.dot(mixed, w_out, preferred_element_type=jnp.float32)

        branch = (
            lax.psum_scatter(
                out_term(jnp.int32(0), lax.axis_size("mp") * share).astype(jnp.bfloat16),
                "mp",
                scatter_dimension=0,
                tiled=True,
            ).astype(jnp.float32)
            + branch_b[0]
        )
        middle = x_rows + normalize(branch, gains[1], shifts[1])
        normed_two = normalize(middle, gains[2], shifts[2]).astype(jnp.bfloat16)
        hidden_two = lax.all_gather(normed_two, "mp", axis=0, tiled=True)
        pre = jnp.dot(hidden_two, w_up, preferred_element_type=jnp.float32) + b_up.astype(
            jnp.float32
        )
        act = gelu_exact(pre).astype(jnp.bfloat16)

        def ffn_term(start, count, act=act, w_down=w_down):
            return jnp.dot(act, w_down, preferred_element_type=jnp.float32)

        ffn_out = (
            lax.psum_scatter(
                ffn_term(jnp.int32(0), lax.axis_size("mp") * share).astype(jnp.bfloat16),
                "mp",
                scatter_dimension=0,
                tiled=True,
            ).astype(jnp.float32)
            + branch_b[1]
        )
        outputs.append((middle + normalize(ffn_out, gains[3], shifts[3])).astype(jnp.bfloat16))
        saved.append(
            (
                x_rows,
                hidden_in,
                q_heads,
                k_heads,
                v_heads,
                log_sums,
                mixed,
                branch,
                middle,
                hidden_two,
                pre,
                act,
                ffn_out,
            )
        )
    grad_inputs = []
    totals = None
    for step in range(batches):
        weights = fetch()
        qkv, qv_b, w_out, w_up, b_up, w_down, gains, shifts, branch_b = weights
        gains = gains.astype(jnp.float32)
        (
            x_rows,
            hidden_in,
            q_heads,
            k_heads,
            v_heads,
            log_sums,
            mixed,
            branch,
            middle,
            hidden_two,
            pre,
            act,
            ffn_out,
        ) = saved[step]
        seg_row = seg_ids[step]
        heads = q_heads.shape[1]
        grad_y = out_grad[step].astype(jnp.float32)
        grad_f, dgain_three, dshift_three = normalize_back(ffn_out, gains[3], grad_y)
        grad_f = grad_f.astype(jnp.bfloat16)
        dbranch_one = jnp.sum(grad_f.astype(jnp.float32), axis=0)
        pull = jax.vjp(gelu_exact, pre)[1]
        grad_f_all = lax.all_gather(grad_f, "mp", axis=0, tiled=True)
        dw_down = jnp.einsum("tf,td->fd", act, grad_f_all, preferred_element_type=jnp.float32)
        grad_act = jnp.einsum("td,fd->tf", grad_f_all, w_down, preferred_element_type=jnp.float32)
        grad_pre = pull(grad_act)[0].astype(jnp.bfloat16)
        dup_bias = jnp.sum(grad_pre.astype(jnp.float32), axis=0)
        dw_up = jnp.einsum("td,tf->df", hidden_two, grad_pre, preferred_element_type=jnp.float32)

        def ffn_back(start, count, grad_pre=grad_pre, w_up=w_up):
            return jnp.einsum("tf,df->td", grad_pre, w_up, preferred_element_type=jnp.float32)

        grad_norm_two = lax.psum_scatter(
            ffn_back(jnp.int32(0), lax.axis_size("mp") * share).astype(jnp.bfloat16),
            "mp",
            scatter_dimension=0,
            tiled=True,
        ).astype(jnp.float32)
        back_two, dgain_two, dshift_two = normalize_back(middle, gains[2], grad_norm_two)
        grad_mid = grad_y + back_two
        grad_branch, dgain_one, dshift_one = normalize_back(branch, gains[1], grad_mid)
        grad_branch = grad_branch.astype(jnp.bfloat16)
        dbranch_zero = jnp.sum(grad_branch.astype(jnp.float32), axis=0)
        grad_branch_all = lax.all_gather(grad_branch, "mp", axis=0, tiled=True)
        dw_out = jnp.einsum("tc,td->cd", mixed, grad_branch_all, preferred_element_type=jnp.float32)
        grad_mixed = jnp.einsum(
            "td,cd->tc", grad_branch_all, w_out, preferred_element_type=jnp.float32
        ).astype(jnp.bfloat16)
        grad_q, grad_k, grad_v = attend_backward(
            q_heads,
            k_heads,
            v_heads,
            seg_row,
            log_sums,
            grad_mixed.reshape(length, heads, HEAD_DIM),
        )
        grad_q = grad_q.reshape(length, heads * HEAD_DIM).astype(jnp.bfloat16)
        grad_k = grad_k.reshape(length, heads * HEAD_DIM).astype(jnp.bfloat16)
        grad_v = grad_v.reshape(length, heads * HEAD_DIM).astype(jnp.bfloat16)
        dw_qkv = jnp.stack(
            [
                scale
                * jnp.einsum("td,tc->dc", hidden_in, grad_q, preferred_element_type=jnp.float32),
                jnp.einsum("td,tc->dc", hidden_in, grad_k, preferred_element_type=jnp.float32),
                jnp.einsum("td,tc->dc", hidden_in, grad_v, preferred_element_type=jnp.float32),
            ]
        )
        dqv_bias = jnp.stack(
            [
                scale * jnp.sum(grad_q.astype(jnp.float32), axis=0),
                jnp.sum(grad_v.astype(jnp.float32), axis=0),
            ]
        )

        def attn_back(start, count, grad_q=grad_q, grad_k=grad_k, grad_v=grad_v, qkv=qkv):
            term = scale * jnp.einsum(
                "tc,dc->td", grad_q, qkv[0], preferred_element_type=jnp.float32
            )
            term = term + jnp.einsum(
                "tc,dc->td", grad_k, qkv[1], preferred_element_type=jnp.float32
            )
            return term + jnp.einsum(
                "tc,dc->td", grad_v, qkv[2], preferred_element_type=jnp.float32
            )

        grad_norm_one = lax.psum_scatter(
            attn_back(jnp.int32(0), lax.axis_size("mp") * share).astype(jnp.bfloat16),
            "mp",
            scatter_dimension=0,
            tiled=True,
        ).astype(jnp.float32)
        back_one, dgain_zero, dshift_zero = normalize_back(x_rows, gains[0], grad_norm_one)
        grad_inputs.append(grad_mid + back_one)
        local = (
            dw_qkv,
            dqv_bias,
            dw_out,
            dw_up,
            dup_bias,
            dw_down,
            jnp.stack([dgain_zero, dgain_one, dgain_two, dgain_three]),
            jnp.stack([dshift_zero, dshift_one, dshift_two, dshift_three]),
            jnp.stack([dbranch_zero, dbranch_one]),
        )
        local = (
            lax.psum_scatter(local[0], "dp", scatter_dimension=1, tiled=True),
            lax.psum_scatter(local[1], "dp", scatter_dimension=1, tiled=True),
            lax.psum_scatter(local[2], "dp", scatter_dimension=0, tiled=True),
            lax.psum_scatter(local[3], "dp", scatter_dimension=0, tiled=True),
            lax.psum_scatter(local[4], "dp", scatter_dimension=0, tiled=True),
            lax.psum_scatter(local[5], "dp", scatter_dimension=0, tiled=True),
            lax.psum_scatter(local[6], "dp", scatter_dimension=1, tiled=True),
            lax.psum_scatter(local[7], "dp", scatter_dimension=1, tiled=True),
            lax.psum_scatter(local[8], "dp", scatter_dimension=1, tiled=True),
        )
        totals = (
            local if totals is None else tuple((left + right for left, right in zip(totals, local)))
        )
    vectors = lax.psum((totals[6], totals[7], totals[8]), "mp")
    return (
        jnp.stack(outputs),
        jnp.stack(grad_inputs),
        totals[0],
        totals[1],
        totals[2],
        totals[3],
        totals[4],
        totals[5],
        vectors[0],
        vectors[1],
        vectors[2],
    )


def solution(mesh):
    in_specs = (
        P(None, ("dp", "mp"), None),
        P(None, "dp"),
        P(None, "dp", "mp"),
        P(None, ("mp", "dp")),
        P(("mp", "dp"), None),
        P("dp", "mp"),
        P(("mp", "dp")),
        P(("mp", "dp"), None),
        P(None, "dp"),
        P(None, "dp"),
        P(None, "dp"),
        P(None, ("dp", "mp"), None),
    )
    out_specs = (
        P(None, ("dp", "mp"), None),
        P(None, ("dp", "mp"), None),
        P(None, "dp", "mp"),
        P(None, ("mp", "dp")),
        P(("mp", "dp"), None),
        P("dp", "mp"),
        P(("mp", "dp")),
        P(("mp", "dp"), None),
        P(None, "dp"),
        P(None, "dp"),
        P(None, "dp"),
    )
    return jax.shard_map(
        on_device, mesh=mesh, in_specs=in_specs, out_specs=out_specs, check_vma=False
    )
```

profile of v0, /device:TPU:0, one launch (start us, length us, event | category | flops | bytes accessed | tf_op | source)
XLA Modules:
  0.0 1328.8 jit_solution(9125537895247549174)
XLA Ops:
  57.2 31.6 %all-gather.24.cloned.1.call-done = bf16[1088,1024]{1,0:T(8,128)(2,1)} async-done(((bf16[272,1024]{1,0:T(8,128)(2,1)}), bf16[1088,1024]{1,0:T(8,128)(2,1)}) %all-gather.24.cloned.1.call-update) | async-done | bytes 2228240 | tf_op jit(solution)/shard_map/all_gather | solution.py:141
  102.0 36.2 %all-gather.14.cloned.1.call-done = bf16[1088,1024]{1,0:T(8,128)(2,1)} async-done(((bf16[272,1024]{1,0:T(8,128)(2,1)}), bf16[1088,1024]{1,0:T(8,128)(2,1)}) %all-gather.14.cloned.1.call-update) | async-done | bytes 2228240 | tf_op jit(solution)/shard_map/all_gather | solution.py:141
  232.2 46.3 %reduce-scatter.29.cloned.1.call-done = bf16[272,1024]{1,0:T(8,128)(2,1)} async-done(((bf16[1088,1024]{1,0:T(8,128)(2,1)}), bf16[272,1024]{1,0:T(8,128)(2,1)}) %reduce-scatter.29.cloned.1.call-update) | async-done | bytes 557072 | tf_op jit(solution)/shard_map/reduce_scatter | solution.py:160
  307.7 50.5 %all-gather.18.cloned.1.call-done = bf16[1088,1024]{1,0:T(8,128)(2,1)} async-done(((bf16[272,1024]{1,0:T(8,128)(2,1)}), bf16[1088,1024]{1,0:T(8,128)(2,1)}) %all-gather.18.cloned.1.call-update) | async-done | bytes 2228240 | tf_op jit(solution)/shard_map/all_gather | solution.py:170
  358.2 15.7 %multiply_convert_fusion.9 = (bf16[1088,1024]{1,0:T(8,128)(2,1)}, f32[1088,1024]{1,0:T(8,128)}, f32[1088,1024]{1,0:T(8,128)}) fusion(f32[1024]{0:T(1024)S(1)} %bitcast.598, bf16[1088,1024]{1,0:T(8,128)(2,1)} %all-gather.18.cloned.1.call-done, bf16[1024,1024]{1,0:T(8,128)(2,1)} %all-gather.20.cloned.1.call-done), kind=kOutput, calls=%fused_computation.77 | convolution fusion | flops 2355232768 | bytes 15470592 | tf_op jit(solution)/shard_map/dot_general | solution.py:171
  393.3 43.5 %all-gather.26.cloned.1.call-done = bf16[1088,1024]{1,0:T(8,128)(2,1)} async-done(((bf16[272,1024]{1,0:T(8,128)(2,1)}), bf16[1088,1024]{1,0:T(8,128)(2,1)}) %all-gather.26.cloned.1.call-update) | async-done | bytes 2228240 | tf_op jit(solution)/shard_map/all_gather | solution.py:170
  436.7 15.5 %multiply_convert_fusion.8 = (bf16[1088,1024]{1,0:T(8,128)(2,1)S(1)}, f32[1088,1024]{1,0:T(8,128)}, f32[1088,1024]{1,0:T(8,128)}) fusion(f32[1024]{0:T(1024)S(1)} %bitcast.599, bf16[1088,1024]{1,0:T(8,128)(2,1)} %all-gather.26.cloned.1.call-done, bf16[1024,1024]{1,0:T(8,128)(2,1)} %all-gather.20.cloned.1.call-done), kind=kOutput, calls=%fused_computation.64 | convolution fusion | flops 2355232768 | bytes 15470592 | tf_op jit(solution)/shard_map/dot_general | solution.py:171
  457.6 26.2 %reduce-scatter.27.cloned.1.call-done = bf16[272,1024]{1,0:T(8,128)(2,1)} async-done(((bf16[1088,1024]{1,0:T(8,128)(2,1)}), bf16[272,1024]{1,0:T(8,128)(2,1)}) %reduce-scatter.27.cloned.1.call-update) | async-done | bytes 557072 | tf_op jit(solution)/shard_map/reduce_scatter | solution.py:180
  485.0 46.5 %reduce-scatter.31.cloned.1.call-done = bf16[272,1024]{1,0:T(8,128)(2,1)} async-done(((bf16[1088,1024]{1,0:T(8,128)(2,1)}), bf16[272,1024]{1,0:T(8,128)(2,1)}) %reduce-scatter.31.cloned.1.call-update) | async-done | bytes 557072 | tf_op jit(solution)/shard_map/reduce_scatter | solution.py:180
  541.3 46.7 %all-gather.28.cloned.1.call-done = bf16[1088,1024]{1,0:T(8,128)(2,1)} async-done(((bf16[272,1024]{1,0:T(8,128)(2,1)}), bf16[1088,1024]{1,0:T(8,128)(2,1)}) %all-gather.28.cloned.1.call-update) | async-done | bytes 2228240 | tf_op jit(solution)/shard_map/all_gather | solution.py:234
  602.7 34.0 %all-gather.32.cloned.1.call-done = bf16[1088,1024]{1,0:T(8,128)(2,1)} async-done(((bf16[272,1024]{1,0:T(8,128)(2,1)}), bf16[1088,1024]{1,0:T(8,128)(2,1)}) %all-gather.32.cloned.1.call-update) | async-done | bytes 2228240 | tf_op jit(solution)/shard_map/all_gather | solution.py:234
  651.6 32.2 %reduce-scatter.33.cloned.1.call-done = bf16[272,1024]{1,0:T(8,128)(2,1)} async-done(((bf16[1088,1024]{1,0:T(8,128)(2,1)}), bf16[272,1024]{1,0:T(8,128)(2,1)}) %reduce-scatter.33.cloned.1.call-update) | async-done | bytes 557072 | tf_op jit(solution)/shard_map/reduce_scatter | solution.py:244
  683.8 47.6 %reduce-scatter.37.cloned.1.call-done = bf16[272,1024]{1,0:T(8,128)(2,1)} async-done(((bf16[1088,1024]{1,0:T(8,128)(2,1)}), bf16[272,1024]{1,0:T(8,128)(2,1)}) %reduce-scatter.37.cloned.1.call-update) | async-done | bytes 557072 | tf_op jit(solution)/shard_map/reduce_scatter | solution.py:244
  742.8 46.9 %all-gather.30.cloned.1.call-done = bf16[1088,1024]{1,0:T(8,128)(2,1)} async-done(((bf16[272,1024]{1,0:T(8,128)(2,1)}), bf16[1088,1024]{1,0:T(8,128)(2,1)}) %all-gather.30.cloned.1.call-update) | async-done | bytes 2228240 | tf_op jit(solution)/shard_map/all_gather | solution.py:255
  802.5 35.8 %all-gather.34.cloned.1.call-done = bf16[1088,1024]{1,0:T(8,128)(2,1)} async-done(((bf16[272,1024]{1,0:T(8,128)(2,1)}), bf16[1088,1024]{1,0:T(8,128)(2,1)}) %all-gather.34.cloned.1.call-update) | async-done | bytes 2228240 | tf_op jit(solution)/shard_map/all_gather | solution.py:255
  936.7 35.9 %reduce-scatter.39.cloned.1.call-done = bf16[272,1024]{1,0:T(8,128)(2,1)} async-done(((bf16[1088,1024]{1,0:T(8,128)(2,1)}), bf16[272,1024]{1,0:T(8,128)(2,1)}) %reduce-scatter.39.cloned.1.call-update) | async-done | bytes 557072 | tf_op jit(solution)/shard_map/reduce_scatter | solution.py:297
  1014.3 13.5 %all-reduce = f32[1024]{0:T(1024)S(1)} all-reduce(f32[1024]{0:T(1024)S(1)} %add.574), channel_id=23, replica_groups=mesh['dp'=8,'mp'=4] {'dp'}, use_global_device_ids=true, to_apply=%region_77.78.clone | all-reduce | flops 1024 | bytes 8192
  1031.6 14.8 %reduce-scatter.49.cloned.1.call-done = f32[32,2]{1,0:T(8,128)} async-done(((f32[256,2]{1,0:T(8,128)}), f32[32,2]{1,0:T(8,128)}) %reduce-scatter.49.cloned.1.call-update) | async-done | bytes 272
  1051.5 32.2 %reduce-scatter.51.cloned.1.call-done = f32[128,4]{1,0:T(8,128)} async-done(((f32[1024,4]{1,0:T(8,128)}), f32[128,4]{1,0:T(8,128)}) %reduce-scatter.51.cloned.1.call-update) | async-done | bytes 2064
  1084.5 36.7 %reduce-scatter.53.cloned.1.call-done = f32[128,4]{1,0:T(8,128)} async-done(((f32[1024,4]{1,0:T(8,128)}), f32[128,4]{1,0:T(8,128)}) %reduce-scatter.53.cloned.1.call-update) | async-done | bytes 2064
  1134.5 41.8 %reduce-scatter.47.cloned.1.call-done = f32[128,1024]{1,0:T(8,128)} async-done(((f32[1024,1024]{1,0:T(8,128)}), f32[128,1024]{1,0:T(8,128)}) %reduce-scatter.47.cloned.1.call-update) | async-done | bytes 524304 | tf_op jit(solution)/shard_map/reduce_scatter | solution.py:322
  1176.3 55.7 %reduce-scatter.45.cloned.1.call-done = f32[128,1024]{1,0:T(8,128)} async-done(((f32[1024,1024]{1,0:T(8,128)}), f32[128,1024]{1,0:T(8,128)}) %reduce-scatter.45.cloned.1.call-update) | async-done | bytes 524304 | tf_op jit(solution)/shard_map/reduce_scatter | solution.py:320
  1232.0 39.7 %reduce-scatter.43.cloned.1.call-done = f32[32,1024]{1,0:T(8,128)} async-done(((f32[256,1024]{1,0:T(8,128)}), f32[32,1024]{1,0:T(8,128)}) %reduce-scatter.43.cloned.1.call-update) | async-done | bytes 131088 | tf_op jit(solution)/shard_map/reduce_scatter | solution.py:319
  1271.7 50.0 %reduce-scatter.41.cloned.1.call-done = f32[3,128,256]{2,1,0:T(8,128)} async-done(((f32[3,1024,256]{2,1,0:T(8,128)}), f32[3,128,256]{2,1,0:T(8,128)}) %reduce-scatter.41.cloned.1.call-update) | async-done | bytes 393232 | tf_op jit(solution)/shard_map/reduce_scatter | solution.py:317
  (687 shorter events, 435.2 us)
Async XLA Ops:
  33.7 104.5 %all-gather.14.cloned.1.call-start = ((), (), s32[]{:S(2)}) async-start(), calls=%async_computation.16 | async-start | bytes 2785280 | tf_op jit(solution)/shard_map/all_gather | solution.py:141
  34.4 196.5 %reduce-scatter.25.cloned.1.call-start = ((), (), s32[]{:S(2)}) async-start(), calls=%async_computation.18 | async-start | bytes 2785280 | tf_op jit(solution)/shard_map/reduce_scatter | solution.py:160
  208.0 99.7 %all-gather.20.cloned.1.call-start = ((), (), s32[]{:S(2)}) async-start(), calls=%async_computation.20 | async-start | bytes 2359296 | tf_op jit(solution)/shard_map/all_gather | solution.py:117
  208.6 149.6 %all-gather.18.cloned.1.call-start = ((), (), s32[]{:S(2)}) async-start(), calls=%async_computation.19 | async-start | bytes 2785280 | tf_op jit(solution)/shard_map/all_gather | solution.py:170
  285.8 101.0 %all-gather.22.cloned.1.call-start = ((), (), s32[]{:S(2)}) async-start(), calls=%async_computation.21 | async-start | bytes 2359296 | tf_op jit(solution)/shard_map/all_gather | solution.py:119
  286.5 150.2 %all-gather.26.cloned.1.call-start = ((), (), s32[]{:S(2)}) async-start(), calls=%async_computation.25 | async-start | bytes 2785280 | tf_op jit(solution)/shard_map/all_gather | solution.py:170
  295.3 188.4 %reduce-scatter.27.cloned.1.call-start = ((), (), s32[]{:S(2)}) async-start(), calls=%async_computation.22 | async-start | bytes 2785280 | tf_op jit(solution)/shard_map/reduce_scatter | solution.py:180
  393.0 138.5 %reduce-scatter.31.cloned.1.call-start = ((), (), s32[]{:S(2)}) async-start(), calls=%async_computation.26 | async-start | bytes 2785280 | tf_op jit(solution)/shard_map/reduce_scatter | solution.py:180
  457.5 130.5 %all-gather.28.cloned.1.call-start = ((), (), s32[]{:S(2)}) async-start(), calls=%async_computation.27 | async-start | bytes 2785280 | tf_op jit(solution)/shard_map/all_gather | solution.py:234
  540.1 96.6 %all-gather.32.cloned.1.call-start = ((), (), s32[]{:S(2)}) async-start(), calls=%async_computation.31 | async-start | bytes 2785280 | tf_op jit(solution)/shard_map/all_gather | solution.py:234
  540.9 142.9 %reduce-scatter.33.cloned.1.call-start = ((), (), s32[]{:S(2)}) async-start(), calls=%async_computation.28 | async-start | bytes 2785280 | tf_op jit(solution)/shard_map/reduce_scatter | solution.py:244
  602.7 128.7 %reduce-scatter.37.cloned.1.call-start = ((), (), s32[]{:S(2)}) async-start(), calls=%async_computation.32 | async-start | bytes 2785280 | tf_op jit(solution)/shard_map/reduce_scatter | solution.py:244
  651.4 138.3 %all-gather.30.cloned.1.call-start = ((), (), s32[]{:S(2)}) async-start(), calls=%async_computation.29 | async-start | bytes 2785280 | tf_op jit(solution)/shard_map/all_gather | solution.py:255
  741.8 96.5 %all-gather.34.cloned.1.call-start = ((), (), s32[]{:S(2)}) async-start(), calls=%async_computation.33 | async-start | bytes 2785280 | tf_op jit(solution)/shard_map/all_gather | solution.py:255
  742.7 194.0 %reduce-scatter.35.cloned.1.call-start = ((), (), s32[]{:S(2)}) async-start(), calls=%async_computation.30 | async-start | bytes 2785280 | tf_op jit(solution)/shard_map/reduce_scatter | solution.py:297
  879.9 92.7 %reduce-scatter.39.cloned.1.call-start = ((), (), s32[]{:S(2)}) async-start(), calls=%async_computation.34 | async-start | bytes 2785280 | tf_op jit(solution)/shard_map/reduce_scatter | solution.py:297
  922.8 108.0 %reduce-scatter.55.cloned.1.call-start = ((), (), s32[]{:S(2)}) async-start(), calls=%async_computation.42 | async-start | bytes 589824
  932.7 113.7 %reduce-scatter.49.cloned.1.call-start = ((), (), s32[]{:S(2)}) async-start(), calls=%async_computation.39 | async-start | bytes 147456
  936.6 147.0 %reduce-scatter.51.cloned.1.call-start = ((), (), s32[]{:S(2)}) async-start(), calls=%async_computation.40 | async-start | bytes 589824
  976.2 145.0 %reduce-scatter.53.cloned.1.call-start = ((), (), s32[]{:S(2)}) async-start(), calls=%async_computation.41 | async-start | bytes 589824
  977.4 198.9 %reduce-scatter.47.cloned.1.call-start = ((), (), s32[]{:S(2)}) async-start(), calls=%async_computation.38 | async-start | bytes 4718592 | tf_op jit(solution)/shard_map/reduce_scatter | solution.py:322
  985.9 246.1 %reduce-scatter.45.cloned.1.call-start = ((), (), s32[]{:S(2)}) async-start(), calls=%async_computation.37 | async-start | bytes 4718592 | tf_op jit(solution)/shard_map/reduce_scatter | solution.py:320
  996.1 275.6 %reduce-scatter.43.cloned.1.call-start = ((), (), s32[]{:S(2)}) async-start(), calls=%async_computation.36 | async-start | bytes 1179648 | tf_op jit(solution)/shard_map/reduce_scatter | solution.py:319
  1001.6 320.1 %reduce-scatter.41.cloned.1.call-start = ((), (), s32[]{:S(2)}) async-start(), calls=%async_computation.35 | async-start | bytes 3538944 | tf_op jit(solution)/shard_map/reduce_scatter | solution.py:317
  (194 other events, 2324.4 us)
Sparse Core Ops, SparseCore 0:
  40.5 48.3 all-gather.23
  91.0 47.1 all-gather.13
  186.1 44.8 reduce-scatter.24
  233.1 45.4 reduce-scatter.28
  309.8 48.3 all-gather.17
  388.4 48.3 all-gather.25
  438.9 44.8 reduce-scatter.26
  486.1 45.4 reduce-scatter.30
  540.3 47.7 all-gather.27
  589.6 47.1 all-gather.31
  638.9 44.8 reduce-scatter.32
  686.0 45.4 reduce-scatter.36
  741.9 47.7 all-gather.29
  791.1 47.1 all-gather.33
  880.0 44.8 reduce-scatter.34
  927.2 45.4 reduce-scatter.38
  976.1 33.5 reduce-scatter.54
  1013.0 33.3 reduce-scatter.48
  1049.5 34.1 reduce-scatter.50
  1087.0 34.1 reduce-scatter.52
  1125.0 51.3 reduce-scatter.46
  1180.6 51.3 reduce-scatter.44
  1235.6 36.0 reduce-scatter.42
  1275.5 46.1 reduce-scatter.40
  (3 shorter events, 82.3 us)
where the time goes:
time: 1330 us
  waiting for transfers between devices  873 us (66%)
  matrix products  222 us (17%)
  blocking collectives  81.3 us (6%)
  other arithmetic  69 us (5%)
  local copies, waits for them, and re-layouts  62.5 us (5%)
  between operations  18.1 us (1%)
    all_gather x2, waiting for transfers between devices, on_device(): hidden_two = lax.all_gather(normed_two, 'mp', axis=0, tiled=True)  94 us
    unnamed x31, waiting for transfers between devices  87.3 us
    all_gather x2, waiting for transfers between devices, on_device(): grad_branch_all = lax.all_gather(grad_branch, 'mp', axis=0, tiled=True)  82.7 us
    all_gather x2, waiting for transfers between devices, on_device(): grad_f_all = lax.all_gather(grad_f, 'mp', axis=0, tiled=True)  80.7 us
    reduce_scatter x2, waiting for transfers between devices, on_device(): lax.psum_scatter(ffn_back(jnp.int32(0), lax.axis_size('mp') * share).asty...  79.8 us
    reduce_scatter x2, waiting for transfers between devices, on_device(): lax.psum_scatter(ffn_term(jnp.int32(0), lax.axis_size('mp') * share).asty...  72.7 us
    all_gather x2, waiting for transfers between devices, on_device(): hidden_in = lax.all_gather(normed, 'mp', axis=0, tiled=True)  67.9 us
    reduce_scatter x2, waiting for transfers between devices, on_device(): lax.psum_scatter(out_term(jnp.int32(0), lax.axis_size('mp') * share).asty...  59.8 us
  transfers between devices with their start and end apart: 27, of which 24 were waited for; matrix products, arithmetic and copies ran while one was open for 17% of the time, Pallas kernels for 0%

commit v1 on v0

--- a/solution.py
+++ b/solution.py
@@ -167,7 +167,14 @@
         )
         middle = x_rows + normalize(branch, gains[1], shifts[1])
         normed_two = normalize(middle, gains[2], shifts[2]).astype(jnp.bfloat16)
-        hidden_two = lax.all_gather(normed_two, "mp", axis=0, tiled=True)
+        ring = [normed_two]
+        for hop in range(3):
+            ring.append(lax.ppermute(ring[-1], "mp", [(dev, (dev + 1) % 4) for dev in range(4)]))
+        hidden_two = jnp.roll(
+            jnp.concatenate(ring[::-1], axis=0),
+            (lax.axis_index("mp") + 1) * ring[0].shape[0],
+            axis=0,
+        )
         pre = jnp.dot(hidden_two, w_up, preferred_element_type=jnp.float32) + b_up.astype(
             jnp.float32
         )

time: 1330 us -> 1280 us (0.962)
  waiting for transfers between devices: 873 us -> 793 us
  other arithmetic: 69 us -> 101 us
    all_gather x2 -> x0, waiting for transfers between devices: 94 us -> none  [on_device(): hidden_two = lax.all_gather(normed_two, 'mp', axis=0, tiled=True)]
    ppermute x0 -> x6, waiting for transfers between devices: none -> 54 us  [on_device(): lax.ppermute(ring[-1], 'mp', [(dev, (dev + 1) % 4) for dev in range(4)])]
    concatenate x0 -> x2, other arithmetic: none -> 21.6 us  [on_device(): jnp.roll(jnp.concatenate(ring[::-1], axis=0), (lax.axis_index('mp') + 1)...]
    unnamed x31 -> x29, waiting for transfers between devices: 87.3 us -> 86 us
    unnamed x392 -> x402, local copies, waits for them, and re-layouts: 28.4 us -> 28.4 us
  transfers between devices with their start and end apart: 27 -> 31, of which waited for: 24 -> 25; matrix products, arithmetic and copies ran while one was open for 17% -> 20% of each run, Pallas kernels for 0% -> 0%
where the time goes in v1:
time: 1280 us; the launch traced here: 1270 us
  waiting for transfers between devices  793 us (62%)
  matrix products  211 us (16%)
  other arithmetic  101 us (8%)
  blocking collectives  81.3 us (6%)
  local copies, waits for them, and re-layouts  62.8 us (5%)
  between operations  17.8 us (1%)
    unnamed x29, waiting for transfers between devices  86 us
    all_gather x2, waiting for transfers between devices, on_device(): grad_branch_all = lax.all_gather(grad_branch, 'mp', axis=0, tiled=True)  82.4 us
    all_gather x2, waiting for transfers between devices, on_device(): grad_f_all = lax.all_gather(grad_f, 'mp', axis=0, tiled=True)  79.8 us
    reduce_scatter x2, waiting for transfers between devices, on_device(): lax.psum_scatter(ffn_back(jnp.int32(0), lax.axis_size('mp') * share).asty...  78.9 us
    all_gather x2, waiting for transfers between devices, on_device(): hidden_in = lax.all_gather(normed, 'mp', axis=0, tiled=True)  67.8 us
    reduce_scatter x2, waiting for transfers between devices, on_device(): lax.psum_scatter(ffn_term(jnp.int32(0), lax.axis_size('mp') * share).asty...  61.1 us
    reduce_scatter x2, waiting for transfers between devices, on_device(): lax.psum_scatter(out_term(jnp.int32(0), lax.axis_size('mp') * share).asty...  59.9 us
    reduce_scatter x1, waiting for transfers between devices, on_device(): lax.psum_scatter(local[3], 'dp', scatter_dimension=0, tiled=True)  55.7 us
  transfers between devices with their start and end apart: 31, of which 25 were waited for; matrix products, arithmetic and copies ran while one was open for 20% of the time, Pallas kernels for 0%

profile of v1, /device:TPU:0, one launch (start us, length us, event | category | flops | bytes accessed | tf_op | source)
XLA Modules:
  0.0 1272.0 jit_solution(6362943127267193362)
XLA Ops:
  57.4 31.5 %all-gather.20.cloned.1.call-done = bf16[1088,1024]{1,0:T(8,128)(2,1)} async-done(((bf16[272,1024]{1,0:T(8,128)(2,1)}), bf16[1088,1024]{1,0:T(8,128)(2,1)}) %all-gather.20.cloned.1.call-update) | async-done | bytes 2228240 | tf_op jit(solution)/shard_map/all_gather | solution.py:141
  101.9 36.3 %all-gather.12.cloned.1.call-done = bf16[1088,1024]{1,0:T(8,128)(2,1)} async-done(((bf16[272,1024]{1,0:T(8,128)(2,1)}), bf16[1088,1024]{1,0:T(8,128)(2,1)}) %all-gather.12.cloned.1.call-update) | async-done | bytes 2228240 | tf_op jit(solution)/shard_map/all_gather | solution.py:141
  217.7 13.6 %reduce-scatter.25.cloned.1.call-done = bf16[272,1024]{1,0:T(8,128)(2,1)} async-done(((bf16[1088,1024]{1,0:T(8,128)(2,1)}), bf16[272,1024]{1,0:T(8,128)(2,1)}) %reduce-scatter.25.cloned.1.call-update) | async-done | bytes 557072 | tf_op jit(solution)/shard_map/reduce_scatter | solution.py:160
  232.5 46.3 %reduce-scatter.29.cloned.1.call-done = bf16[272,1024]{1,0:T(8,128)(2,1)} async-done(((bf16[1088,1024]{1,0:T(8,128)(2,1)}), bf16[272,1024]{1,0:T(8,128)(2,1)}) %reduce-scatter.29.cloned.1.call-update) | async-done | bytes 557072 | tf_op jit(solution)/shard_map/reduce_scatter | solution.py:160
  287.5 15.0 %collective-permute-done = bf16[272,1024]{1,0:T(8,128)(2,1)S(1)} collective-permute-done((bf16[272,1024]{1,0:T(8,128)(2,1)S(1)}, bf16[272,1024]{1,0:T(8,128)(2,1)S(1)}, u32[]{:S(2)}, u32[]{:S(2)}) %collective-permute-start) | collective-permute-done | bytes 557088 | tf_op jit(solution)/shard_map/ppermute | solution.py:172
  361.6 15.7 %multiply_convert_fusion.9 = (bf16[1088,1024]{1,0:T(8,128)(2,1)}, f32[1088,1024]{1,0:T(8,128)}, f32[1088,1024]{1,0:T(8,128)}) fusion(f32[1024]{0:T(1024)S(1)} %bitcast.598, bf16[1088,1024]{1,0:T(8,128)(2,1)} %fusion.84, bf16[1024,1024]{1,0:T(8,128)(2,1)} %all-gather.16.cloned.1.call-done), kind=kOutput, calls=%fused_computation.93 | convolution fusion | flops 2355232768 | bytes 15470592 | tf_op jit(solution)/shard_map/dot_general | solution.py:178
  394.2 13.3 %multiply_convert_fusion.8 = (bf16[1088,1024]{1,0:T(8,128)(2,1)S(1)}, f32[1088,1024]{1,0:T(8,128)}, f32[1088,1024]{1,0:T(8,128)}) fusion(f32[1024]{0:T(1024)S(1)} %bitcast.599, bf16[1088,1024]{1,0:T(8,128)(2,1)S(1)} %fusion.77, bf16[1024,1024]{1,0:T(8,128)(2,1)S(1)} %copy-done.166), kind=kOutput, calls=%fused_computation.80 | convolution fusion | flops 2355232768 | bytes 15470592 | tf_op jit(solution)/shard_map/dot_general | solution.py:178
  413.1 14.6 %reduce-scatter.27.cloned.1.call-done = bf16[272,1024]{1,0:T(8,128)(2,1)} async-done(((bf16[1088,1024]{1,0:T(8,128)(2,1)}), bf16[272,1024]{1,0:T(8,128)(2,1)}) %reduce-scatter.27.cloned.1.call-update) | async-done | bytes 557072 | tf_op jit(solution)/shard_map/reduce_scatter | solution.py:187
  429.0 46.5 %reduce-scatter.31.cloned.1.call-done = bf16[272,1024]{1,0:T(8,128)(2,1)} async-done(((bf16[1088,1024]{1,0:T(8,128)(2,1)}), bf16[272,1024]{1,0:T(8,128)(2,1)}) %reduce-scatter.31.cloned.1.call-update) | async-done | bytes 557072 | tf_op jit(solution)/shard_map/reduce_scatter | solution.py:187
  484.9 47.1 %all-gather.26.cloned.1.call-done = bf16[1088,1024]{1,0:T(8,128)(2,1)} async-done(((bf16[272,1024]{1,0:T(8,128)(2,1)}), bf16[1088,1024]{1,0:T(8,128)(2,1)}) %all-gather.26.cloned.1.call-update) | async-done | bytes 2228240 | tf_op jit(solution)/shard_map/all_gather | solution.py:241
  548.0 32.7 %all-gather.22.cloned.1.call-done = bf16[1088,1024]{1,0:T(8,128)(2,1)} async-done(((bf16[272,1024]{1,0:T(8,128)(2,1)}), bf16[1088,1024]{1,0:T(8,128)(2,1)}) %all-gather.22.cloned.1.call-update) | async-done | bytes 2228240 | tf_op jit(solution)/shard_map/all_gather | solution.py:241
  596.6 31.1 %reduce-scatter.37.cloned.1.call-done = bf16[272,1024]{1,0:T(8,128)(2,1)} async-done(((bf16[1088,1024]{1,0:T(8,128)(2,1)}), bf16[272,1024]{1,0:T(8,128)(2,1)}) %reduce-scatter.37.cloned.1.call-update) | async-done | bytes 557072 | tf_op jit(solution)/shard_map/reduce_scatter | solution.py:251
  627.8 47.8 %reduce-scatter.33.cloned.1.call-done = bf16[272,1024]{1,0:T(8,128)(2,1)} async-done(((bf16[1088,1024]{1,0:T(8,128)(2,1)}), bf16[272,1024]{1,0:T(8,128)(2,1)}) %reduce-scatter.33.cloned.1.call-update) | async-done | bytes 557072 | tf_op jit(solution)/shard_map/reduce_scatter | solution.py:251
  686.9 46.9 %all-gather.24.cloned.1.call-done = bf16[1088,1024]{1,0:T(8,128)(2,1)} async-done(((bf16[272,1024]{1,0:T(8,128)(2,1)}), bf16[1088,1024]{1,0:T(8,128)(2,1)}) %all-gather.24.cloned.1.call-update) | async-done | bytes 2228240 | tf_op jit(solution)/shard_map/all_gather | solution.py:262
  746.9 35.5 %all-gather.28.cloned.1.call-done = bf16[1088,1024]{1,0:T(8,128)(2,1)} async-done(((bf16[272,1024]{1,0:T(8,128)(2,1)}), bf16[1088,1024]{1,0:T(8,128)(2,1)}) %all-gather.28.cloned.1.call-update) | async-done | bytes 2228240 | tf_op jit(solution)/shard_map/all_gather | solution.py:262
  880.7 35.8 %reduce-scatter.39.cloned.1.call-done = bf16[272,1024]{1,0:T(8,128)(2,1)} async-done(((bf16[1088,1024]{1,0:T(8,128)(2,1)}), bf16[272,1024]{1,0:T(8,128)(2,1)}) %reduce-scatter.39.cloned.1.call-update) | async-done | bytes 557072 | tf_op jit(solution)/shard_map/reduce_scatter | solution.py:304
  958.2 13.5 %all-reduce = f32[1024]{0:T(1024)S(1)} all-reduce(f32[1024]{0:T(1024)S(1)} %add.589), channel_id=23, replica_groups=mesh['dp'=8,'mp'=4] {'dp'}, use_global_device_ids=true, to_apply=%region_77.79.clone | all-reduce | flops 1024 | bytes 8192
  975.4 14.3 %reduce-scatter.49.cloned.1.call-done = f32[32,2]{1,0:T(8,128)} async-done(((f32[256,2]{1,0:T(8,128)}), f32[32,2]{1,0:T(8,128)}) %reduce-scatter.49.cloned.1.call-update) | async-done | bytes 272
  994.8 32.1 %reduce-scatter.51.cloned.1.call-done = f32[128,4]{1,0:T(8,128)} async-done(((f32[1024,4]{1,0:T(8,128)}), f32[128,4]{1,0:T(8,128)}) %reduce-scatter.51.cloned.1.call-update) | async-done | bytes 2064
  1027.8 36.7 %reduce-scatter.53.cloned.1.call-done = f32[128,4]{1,0:T(8,128)} async-done(((f32[1024,4]{1,0:T(8,128)}), f32[128,4]{1,0:T(8,128)}) %reduce-scatter.53.cloned.1.call-update) | async-done | bytes 2064
  1077.7 42.0 %reduce-scatter.47.cloned.1.call-done = f32[128,1024]{1,0:T(8,128)} async-done(((f32[1024,1024]{1,0:T(8,128)}), f32[128,1024]{1,0:T(8,128)}) %reduce-scatter.47.cloned.1.call-update) | async-done | bytes 524304 | tf_op jit(solution)/shard_map/reduce_scatter | solution.py:329
  1119.7 55.7 %reduce-scatter.45.cloned.1.call-done = f32[128,1024]{1,0:T(8,128)} async-done(((f32[1024,1024]{1,0:T(8,128)}), f32[128,1024]{1,0:T(8,128)}) %reduce-scatter.45.cloned.1.call-update) | async-done | bytes 524304 | tf_op jit(solution)/shard_map/reduce_scatter | solution.py:327
  1175.4 39.7 %reduce-scatter.43.cloned.1.call-done = f32[32,1024]{1,0:T(8,128)} async-done(((f32[256,1024]{1,0:T(8,128)}), f32[32,1024]{1,0:T(8,128)}) %reduce-scatter.43.cloned.1.call-update) | async-done | bytes 131088 | tf_op jit(solution)/shard_map/reduce_scatter | solution.py:326
  1215.0 50.2 %reduce-scatter.41.cloned.1.call-done = f32[3,128,256]{2,1,0:T(8,128)} async-done(((f32[3,1024,256]{2,1,0:T(8,128)}), f32[3,128,256]{2,1,0:T(8,128)}) %reduce-scatter.41.cloned.1.call-update) | async-done | bytes 393232 | tf_op jit(solution)/shard_map/reduce_scatter | solution.py:324
  (707 shorter events, 460.3 us)
Async XLA Ops:
  7.9 81.0 %all-gather.20.cloned.1.call-start = ((), (), s32[]{:S(2)}) async-start(), calls=%async_computation.22 | async-start | bytes 2785280 | tf_op jit(solution)/shard_map/all_gather | solution.py:141
  33.7 104.5 %all-gather.12.cloned.1.call-start = ((), (), s32[]{:S(2)}) async-start(), calls=%async_computation.16 | async-start | bytes 2785280 | tf_op jit(solution)/shard_map/all_gather | solution.py:141
  34.4 196.8 %reduce-scatter.25.cloned.1.call-start = ((), (), s32[]{:S(2)}) async-start(), calls=%async_computation.18 | async-start | bytes 2785280 | tf_op jit(solution)/shard_map/reduce_scatter | solution.py:160
  186.3 92.6 %reduce-scatter.29.cloned.1.call-start = ((), (), s32[]{:S(2)}) async-start(), calls=%async_computation.23 | async-start | bytes 2785280 | tf_op jit(solution)/shard_map/reduce_scatter | solution.py:160
  208.1 153.5 %all-gather.16.cloned.1.call-start = ((), (), s32[]{:S(2)}) async-start(), calls=%async_computation.19 | async-start | bytes 2359296 | tf_op jit(solution)/shard_map/all_gather | solution.py:117
  208.7 168.6 %all-gather.18.cloned.1.call-start = ((), (), s32[]{:S(2)}) async-start(), calls=%async_computation.20 | async-start | bytes 2359296 | tf_op jit(solution)/shard_map/all_gather | solution.py:119
  326.5 101.2 %reduce-scatter.27.cloned.1.call-start = ((), (), s32[]{:S(2)}) async-start(), calls=%async_computation.21 | async-start | bytes 2785280 | tf_op jit(solution)/shard_map/reduce_scatter | solution.py:187
  383.4 92.1 %reduce-scatter.31.cloned.1.call-start = ((), (), s32[]{:S(2)}) async-start(), calls=%async_computation.24 | async-start | bytes 2785280 | tf_op jit(solution)/shard_map/reduce_scatter | solution.py:187
  412.8 119.2 %all-gather.26.cloned.1.call-start = ((), (), s32[]{:S(2)}) async-start(), calls=%async_computation.29 | async-start | bytes 2785280 | tf_op jit(solution)/shard_map/all_gather | solution.py:241
  484.1 96.7 %all-gather.22.cloned.1.call-start = ((), (), s32[]{:S(2)}) async-start(), calls=%async_computation.25 | async-start | bytes 2785280 | tf_op jit(solution)/shard_map/all_gather | solution.py:241
  484.8 142.9 %reduce-scatter.37.cloned.1.call-start = ((), (), s32[]{:S(2)}) async-start(), calls=%async_computation.30 | async-start | bytes 2785280 | tf_op jit(solution)/shard_map/reduce_scatter | solution.py:251
  547.8 127.8 %reduce-scatter.33.cloned.1.call-start = ((), (), s32[]{:S(2)}) async-start(), calls=%async_computation.26 | async-start | bytes 2785280 | tf_op jit(solution)/shard_map/reduce_scatter | solution.py:251
  596.6 137.2 %all-gather.24.cloned.1.call-start = ((), (), s32[]{:S(2)}) async-start(), calls=%async_computation.27 | async-start | bytes 2785280 | tf_op jit(solution)/shard_map/all_gather | solution.py:262
  685.9 96.5 %all-gather.28.cloned.1.call-start = ((), (), s32[]{:S(2)}) async-start(), calls=%async_computation.31 | async-start | bytes 2785280 | tf_op jit(solution)/shard_map/all_gather | solution.py:262
  686.8 193.9 %reduce-scatter.35.cloned.1.call-start = ((), (), s32[]{:S(2)}) async-start(), calls=%async_computation.28 | async-start | bytes 2785280 | tf_op jit(solution)/shard_map/reduce_scatter | solution.py:304
  824.0 92.6 %reduce-scatter.39.cloned.1.call-start = ((), (), s32[]{:S(2)}) async-start(), calls=%async_computation.32 | async-start | bytes 2785280 | tf_op jit(solution)/shard_map/reduce_scatter | solution.py:304
  866.8 107.7 %reduce-scatter.55.cloned.1.call-start = ((), (), s32[]{:S(2)}) async-start(), calls=%async_computation.40 | async-start | bytes 589824
  876.8 113.0 %reduce-scatter.49.cloned.1.call-start = ((), (), s32[]{:S(2)}) async-start(), calls=%async_computation.37 | async-start | bytes 147456
  880.7 146.2 %reduce-scatter.51.cloned.1.call-start = ((), (), s32[]{:S(2)}) async-start(), calls=%async_computation.38 | async-start | bytes 589824
  920.1 144.3 %reduce-scatter.53.cloned.1.call-start = ((), (), s32[]{:S(2)}) async-start(), calls=%async_computation.39 | async-start | bytes 589824
  921.3 198.4 %reduce-scatter.47.cloned.1.call-start = ((), (), s32[]{:S(2)}) async-start(), calls=%async_computation.36 | async-start | bytes 4718592 | tf_op jit(solution)/shard_map/reduce_scatter | solution.py:329
  929.8 245.5 %reduce-scatter.45.cloned.1.call-start = ((), (), s32[]{:S(2)}) async-start(), calls=%async_computation.35 | async-start | bytes 4718592 | tf_op jit(solution)/shard_map/reduce_scatter | solution.py:327
  940.0 275.1 %reduce-scatter.43.cloned.1.call-start = ((), (), s32[]{:S(2)}) async-start(), calls=%async_computation.34 | async-start | bytes 1179648 | tf_op jit(solution)/shard_map/reduce_scatter | solution.py:326
  945.5 319.7 %reduce-scatter.41.cloned.1.call-start = ((), (), s32[]{:S(2)}) async-start(), calls=%async_computation.33 | async-start | bytes 3538944 | tf_op jit(solution)/shard_map/reduce_scatter | solution.py:324
  (203 other events, 2365.7 us)
Sparse Core Ops, SparseCore 0:
  9.9 28.3 all-gather.13
  40.5 48.3 all-gather.19
  91.0 47.1 all-gather.11
  186.4 44.8 reduce-scatter.24
  233.4 45.4 reduce-scatter.28
  326.6 29.2 all-gather.17
  383.5 44.1 reduce-scatter.26
  430.0 45.4 reduce-scatter.30
  484.2 47.7 all-gather.25
  533.6 47.1 all-gather.21
  582.9 44.8 reduce-scatter.36
  630.1 45.4 reduce-scatter.32
  686.0 47.7 all-gather.23
  735.2 47.1 all-gather.27
  824.1 44.8 reduce-scatter.34
  871.1 45.4 reduce-scatter.38
  919.5 33.5 reduce-scatter.54
  956.4 33.3 reduce-scatter.48
  992.7 34.1 reduce-scatter.50
  1030.3 34.1 reduce-scatter.52
  1068.4 51.3 reduce-scatter.46
  1124.0 51.3 reduce-scatter.44
  1179.0 36.0 reduce-scatter.42
  1219.0 46.1 reduce-scatter.40
  (1 shorter events, 27.2 us)
